TPU v7x, 32 devices: a whole 2x2x4 slice. The times are simulated.
32 devices in a mesh: prow: 8 (over z, y), pcol: 4 (over x, core).
Axes of the slice: x: 2, y: 2, z: 4, core: 2. Of those that a mesh axis runs over, the one named last changes fastest.
Arguments:
- a_panel: float32 [98304, 512], P('prow', 'pcol'), may hold values from -6 to 6
- u_rows: float32 [512, 98304], P('pcol', 'prow'), may hold values from -0.25 to 0.25
- u_col: float32 [98304, 2048], P('prow', 'pcol'), may hold values from -0.01953125 to 0.01953125
- c_in: float32 [98304, 2048], P('prow', 'pcol'), may hold values from -6 to 6
Outputs:
- c_out: float32 [98304, 2048], P('prow', 'pcol')
All inputs are finite; a program needn't handle non-finite values.
Results may differ from a plain program's by a relative error of at most 0.00007.
Values sent between devices are 32-bit elements; how exact they have to be, the bound alone decides.
A program may use at most 192 MiB of HBM per device.

v0:
```python
import jax
import jax.numpy as jnp
from jax import lax
from jax.sharding import PartitionSpec as P


def gather_later(u_rows):
    return lax.all_gather(u_rows, "pcol", axis=0, tiled=True)


def on_device(a_panel, u_rows, u_col, c_in):
    a_full = lax.all_gather(a_panel, "pcol", axis=1, tiled=True)
    partial_inner = jnp.dot(
        a_full.T, u_col, precision=lax.Precision.HIGHEST, preferred_element_type=jnp.float32
    )
    inner = lax.psum(partial_inner, "prow")
    u_full = gather_later(u_rows)
    result = c_in + jnp.dot(
        u_full.T, inner, precision=lax.Precision.HIGHEST, preferred_element_type=jnp.float32
    )
    return result


def solution(mesh):
    placed = (P("prow", "pcol"), P("pcol", "prow"), P("prow", "pcol"), P("prow", "pcol"))
    return jax.shard_map(
        on_device, mesh=mesh, in_specs=placed, out_specs=P("prow", "pcol"), check_vma=False
    )
```

profile of v0, /device:TPU:0, one launch (start us, length us, event | category | flops | bytes accessed | tf_op | source)
XLA Modules:
  0.0 486.4 jit_solution(6694891880605975887)
XLA Ops:
  6.5 0.0 all-gather.3.cloned.1.call-start
  6.5 0.7 all-gather.3.cloned.1.call-update
  7.3 0.0 all-gather.5.cloned.1.call-start
  7.3 0.7 all-gather.5.cloned.1.call-update
  8.0 0.0 all-reduce.2.cloned.1.call-start
  8.1 161.7 %all-gather.3.cloned.1.call-done = f32[12288,512]{1,0:T(8,128)} async-done(((f32[12288,128]{1,0:T(8,128)}), f32[12288,512]{1,0:T(8,128)}) %all-gather.3.cloned.1.call-update) | async-done | bytes 25165840 | tf_op jit(solution)/shard_map/all_gather | solution.py:12
  169.8 45.2 %fusion = f32[512,512]{1,0:T(8,128)} fusion(f32[12288,512]{1,0:T(8,128)} %all-gather.3.cloned.1.call-done, f32[12288,512]{1,0:T(8,128)} %param.6), kind=kOutput, calls=%fused_computation.1 | convolution fusion | flops 38654705664 | bytes 51380224 | tf_op jit(solution)/shard_map/dot_general | solution.py:13
  215.0 0.0 all-reduce.2.cloned.1.call-update
  215.0 24.7 %copy.5 = f32[12288,512]{0,1:T(8,128)} copy(f32[12288,512]{1,0:T(8,128)} %param.7) | data formatting | bytes 50331648 | tf_op args[3]
  239.7 86.5 %all-gather.5.cloned.1.call-done = f32[512,12288]{1,0:T(8,128)} async-done(((f32[128,12288]{1,0:T(8,128)}), f32[512,12288]{1,0:T(8,128)}) %all-gather.5.cloned.1.call-update) | async-done | bytes 25165840 | tf_op jit(solution)/shard_map/all_gather | solution.py:8
  326.2 81.8 %all-reduce.2.cloned.1.call-done = f32[512,512]{1,0:T(8,128)} async-done(((f32[512,512]{1,0:T(8,128)}), f32[512,512]{1,0:T(8,128)}) %all-reduce.2.cloned.1.call-update) | async-done | bytes 1048592 | tf_op jit(solution)/shard_map/psum | solution.py:16
  407.9 47.2 %bitcast_add_fusion = f32[12288,512]{0,1:T(8,128)} fusion(f32[12288,512]{0,1:T(8,128)} %copy.5, f32[512,512]{1,0:T(8,128)} %all-reduce.2.cloned.1.call-done, f32[512,12288]{1,0:T(8,128)} %all-gather.5.cloned.1.call-done), kind=kOutput, calls=%fused_computation | convolution fusion | flops 38660997120 | bytes 76546048 | tf_op jit(solution)/shard_map/dot_general | solution.py:18
  455.2 24.7 %copy.6 = f32[12288,512]{1,0:T(8,128)} copy(f32[12288,512]{0,1:T(8,128)} %bitcast_add_fusion) | data formatting | bytes 50331648 | tf_op jit(solution)/shard_map/add | solution.py:18
Async XLA Ops:
  6.5 163.3 %all-gather.3.cloned.1.call-start = ((), (), s32[]{:S(2)}) async-start(), calls=%async_computation | async-start | bytes 31457280 | tf_op jit(solution)/shard_map/all_gather | solution.py:12
  7.3 318.9 %all-gather.5.cloned.1.call-start = ((), (), s32[]{:S(2)}) async-start(), calls=%async_computation.2 | async-start | bytes 31457280 | tf_op jit(solution)/shard_map/all_gather | solution.py:8
  8.0 399.9 %all-reduce.2.cloned.1.call-start = ((), (), s32[]{:S(2)}) async-start(), calls=%async_computation.1 | async-start | bytes 2097152 | tf_op jit(solution)/shard_map/psum | solution.py:16
Sparse Core Ops, SparseCore 0:
  8.9 160.8 all-gather.2
  171.4 154.7 all-gather.4
  329.7 78.1 all-reduce.1
where the time goes:
time: 487 us; the launch traced here: 486 us
  waiting for transfers between devices  331 us (68%)
  matrix products  92.4 us (19%)
  local copies, waits for them, and re-layouts  49.4 us (10%)
  between operations  13.1 us (3%)
    all_gather x1, waiting for transfers between devices, on_device(): a_full = lax.all_gather(a_panel, 'pcol', axis=1, tiled=True)  162 us
    all_gather x1, waiting for transfers between devices, gather_later(): return lax.all_gather(u_rows, 'pcol', axis=0, tiled=True)  86.5 us
    psum x1, waiting for transfers between devices, on_device(): inner = lax.psum(partial_inner, 'prow')  81.8 us
    dot_general x1, matrix products, on_device(): jnp.dot(u_full.T, inner, precision=lax.Precision.HIGHEST, preferred_eleme...  47.2 us
    dot_general x1, matrix products, on_device(): jnp.dot(a_full.T, u_col, precision=lax.Precision.HIGHEST, preferred_eleme...  45.2 us
    unnamed x1, local copies, waits for them, and re-layouts  24.7 us
    add x1, local copies, waits for them, and re-layouts, on_device(): c_in + jnp.dot(u_full.T, inner, precision=lax.Precision.HIGHEST, preferre...  24.7 us
  transfers between devices with their start and end apart: 3, of which 3 were waited for; matrix products, arithmetic and copies ran while one was open for 14% of the time, Pallas kernels for 0%

commit v1 on v0

--- a/solution.py
+++ b/solution.py
@@ -13,7 +13,9 @@
     partial_inner = jnp.dot(
         a_full.T, u_col, precision=lax.Precision.HIGHEST, preferred_element_type=jnp.float32
     )
-    inner = lax.psum(partial_inner, "prow")
+    inner = partial_inner
+    for hop in (1, 2, 4):
+        inner = inner + lax.ppermute(inner, "prow", [(dev, dev ^ hop) for dev in range(8)])
     u_full = gather_later(u_rows)
     result = c_in + jnp.dot(
         u_full.T, inner, precision=lax.Precision.HIGHEST, preferred_element_type=jnp.float32

time: 487 us -> 406 us (0.83)
  waiting for transfers between devices: 331 us -> 245 us
  starting transfers between devices: 0.08 us -> 5.59 us
    psum x1 -> x0, waiting for transfers between devices: 81.8 us -> none  [on_device(): inner = lax.psum(partial_inner, 'prow')]
    all_gather x1, waiting for transfers between devices: 86.5 us -> 34.5 us  [gather_later(): return lax.all_gather(u_rows, 'pcol', axis=0, tiled=True)]
    ppermute x0 -> x3, waiting for transfers between devices: none -> 46.9 us  [on_device(): lax.ppermute(inner, 'prow', [(dev, dev ^ hop) for dev in range(8)])]
    ppermute x0 -> x3, starting transfers between devices: none -> 5.55 us  [on_device(): lax.ppermute(inner, 'prow', [(dev, dev ^ hop) for dev in range(8)])]
  transfers between devices with their start and end apart: 3 -> 5, of which waited for: 3 -> 4; matrix products, arithmetic and copies ran while one was open for 14% -> 17% of each run, Pallas kernels for 0% -> 0%
where the time goes in v1:
time: 406 us; the launch traced here: 405 us
  waiting for transfers between devices  245 us (60%)
  matrix products  91.5 us (23%)
  local copies, waits for them, and re-layouts  49.4 us (12%)
  between operations  13.4 us (3%)
  starting transfers between devices  5.59 us (1%)
    all_gather x1, waiting for transfers between devices, on_device(): a_full = lax.all_gather(a_panel, 'pcol', axis=1, tiled=True)  162 us
    dot_general x1, matrix products, on_device(): jnp.dot(u_full.T, inner, precision=lax.Precision.HIGHEST, preferred_eleme...  47.2 us
    ppermute x3, waiting for transfers between devices, on_device(): lax.ppermute(inner, 'prow', [(dev, dev ^ hop) for dev in range(8)])  46.9 us
    dot_general x1, matrix products, on_device(): jnp.dot(a_full.T, u_col, precision=lax.Precision.HIGHEST, preferred_eleme...  44.3 us
    all_gather x1, waiting for transfers between devices, gather_later(): return lax.all_gather(u_rows, 'pcol', axis=0, tiled=True)  34.5 us
    unnamed x1, local copies, waits for them, and re-layouts  24.7 us
    add x1, local copies, waits for them, and re-layouts, on_device(): c_in + jnp.dot(u_full.T, inner, precision=lax.Precision.HIGHEST, preferre...  24.7 us
  transfers between devices with their start and end apart: 5, of which 4 were waited for; matrix products, arithmetic and copies ran while one was open for 17% of the time, Pallas kernels for 0%

profile of v1, /device:TPU:0, one launch (start us, length us, event | category | flops | bytes accessed | tf_op | source)
XLA Modules:
  0.0 404.9 jit_solution(9674740499030536314)
XLA Ops:
  6.5 0.0 all-gather.3.cloned.1.call-start
  6.5 0.7 all-gather.3.cloned.1.call-update
  7.3 0.0 all-gather.5.cloned.1.call-start
  7.3 0.7 all-gather.5.cloned.1.call-update
  8.0 161.8 %all-gather.3.cloned.1.call-done = f32[12288,512]{1,0:T(8,128)} async-done(((f32[12288,128]{1,0:T(8,128)}), f32[12288,512]{1,0:T(8,128)}) %all-gather.3.cloned.1.call-update) | async-done | bytes 25165840 | tf_op jit(solution)/shard_map/all_gather | solution.py:12
  169.8 44.3 %fusion.1 = f32[512,512]{1,0:T(8,128)S(1)} fusion(f32[12288,512]{1,0:T(8,128)} %all-gather.3.cloned.1.call-done, f32[12288,512]{1,0:T(8,128)} %param.6), kind=kOutput, calls=%fused_computation.2 | convolution fusion | flops 38654705664 | bytes 51380224 | tf_op jit(solution)/shard_map/dot_general | solution.py:13
  214.1 1.5 collective-permute-start
  215.6 23.8 %collective-permute-done = f32[512,512]{1,0:T(8,128)S(1)} collective-permute-done((f32[512,512]{1,0:T(8,128)S(1)}, f32[512,512]{1,0:T(8,128)S(1)}, u32[]{:S(2)}, u32[]{:S(2)}) %collective-permute-start) | collective-permute-done | bytes 1048608 | tf_op jit(solution)/shard_map/ppermute | solution.py:18
  239.5 0.2 add.12
  239.7 1.6 collective-permute-start.1
  241.2 23.1 %collective-permute-done.1 = f32[512,512]{1,0:T(8,128)S(1)} collective-permute-done((f32[512,512]{1,0:T(8,128)S(1)}, f32[512,512]{1,0:T(8,128)S(1)}, u32[]{:S(2)}, u32[]{:S(2)}) %collective-permute-start.1) | collective-permute-done | bytes 1048608 | tf_op jit(solution)/shard_map/ppermute | solution.py:18
  264.3 0.2 add.13
  264.5 2.5 collective-permute-start.2
  267.0 24.7 %copy.5 = f32[12288,512]{0,1:T(8,128)} copy(f32[12288,512]{1,0:T(8,128)} %param.7) | data formatting | bytes 50331648 | tf_op args[3]
  291.7 34.5 %all-gather.5.cloned.1.call-done = f32[512,12288]{1,0:T(8,128)} async-done(((f32[128,12288]{1,0:T(8,128)}), f32[512,12288]{1,0:T(8,128)}) %all-gather.5.cloned.1.call-update) | async-done | bytes 25165840 | tf_op jit(solution)/shard_map/all_gather | solution.py:8
  326.2 0.0 collective-permute-done.2
  326.2 47.2 %bitcast_add_fusion = f32[12288,512]{0,1:T(8,128)} fusion(f32[12288,512]{0,1:T(8,128)} %copy.5, f32[512,12288]{1,0:T(8,128)} %all-gather.5.cloned.1.call-done, f32[512,512]{1,0:T(8,128)S(1)} %add.13, f32[512,512]{1,0:T(8,128)S(1)} %collective-permute-done.2), kind=kOutput, calls=%fused_computation | convolution fusion | flops 38661259264 | bytes 77594624 | tf_op jit(solution)/shard_map/dot_general | solution.py:20
  373.4 24.7 %copy.6 = f32[12288,512]{1,0:T(8,128)} copy(f32[12288,512]{0,1:T(8,128)} %bitcast_add_fusion) | data formatting | bytes 50331648 | tf_op jit(solution)/shard_map/add | solution.py:20
Async XLA Ops:
  6.5 163.3 %all-gather.3.cloned.1.call-start = ((), (), s32[]{:S(2)}) async-start(), calls=%async_computation | async-start | bytes 31457280 | tf_op jit(solution)/shard_map/all_gather | solution.py:12
  7.3 318.9 %all-gather.5.cloned.1.call-start = ((), (), s32[]{:S(2)}) async-start(), calls=%async_computation.1 | async-start | bytes 31457280 | tf_op jit(solution)/shard_map/all_gather | solution.py:8
  214.1 25.4 %collective-permute-start = (f32[512,512]{1,0:T(8,128)S(1)}, f32[512,512]{1,0:T(8,128)S(1)}, u32[]{:S(2)}, u32[]{:S(2)}) collective-permute-start(f32[512,512]{1,0:T(8,128)S(1)} %fusion.1), channel_id=1, source_target_pairs={{0,4},{4,0},{8,12},{12,8},{16,20},{20,16},{24,28},{28,24},{1,5},{5... | collective-permute-start | bytes 3145736 | tf_op jit(solution)/shard_map/ppermute | solution.py:18
  239.7 24.6 %collective-permute-start.1 = (f32[512,512]{1,0:T(8,128)S(1)}, f32[512,512]{1,0:T(8,128)S(1)}, u32[]{:S(2)}, u32[]{:S(2)}) collective-permute-start(f32[512,512]{1,0:T(8,128)S(1)} %add.12), channel_id=1, source_target_pairs={{0,8},{4,12},{8,0},{12,4},{16,24},{20,28},{24,16},{28,20},{1,9},{5... | collective-permute-start | bytes 3145736 | tf_op jit(solution)/shard_map/ppermute | solution.py:18
  264.5 61.7 %collective-permute-start.2 = (f32[512,512]{1,0:T(8,128)S(1)}, f32[512,512]{1,0:T(8,128)S(1)}, u32[]{:S(2)}, u32[]{:S(2)}) collective-permute-start(f32[512,512]{1,0:T(8,128)S(1)} %add.13), channel_id=1, source_target_pairs={{0,16},{4,20},{8,24},{12,28},{16,0},{20,4},{24,8},{28,12},{1,17},{... | collective-permute-start | bytes 3145736 | tf_op jit(solution)/shard_map/ppermute | solution.py:18
Sparse Core Ops, SparseCore 0:
  8.9 160.8 all-gather.2
  171.4 154.7 all-gather.4
